TPU v7x, 32 devices: a whole 2x2x4 slice. The times are simulated.
32 devices in a mesh: seq: 4 (over z), mp: 8 (over y, x, core).
Axes of the slice: x: 2, y: 2, z: 4, core: 2. Of those that a mesh axis runs over, the one named last changes fastest.
Arguments:
- ids: int32 [16, 1024], P('seq'), may hold values from 0 to 274
- lengths: int32 [1024], replicated, may hold values from 1 to 16, 12288 in all
- order: int32 [1024], replicated, may hold values from 0 to 1023, each once
- h_init: bfloat16 [2, 1024, 2048], P(None, 'seq', 'mp'), may hold values from -3 to 3
- c_init: float32 [2, 1024, 2048], P(None, 'seq', 'mp'), may hold values from -5 to 5
- embed: bfloat16 [2, 275, 100], replicated, may hold values from -5 to 5
- w_in: bfloat16 [2, 100, 8192], P(None, None, 'mp'), may hold values from -0.625 to 0.625
- w_rec: bfloat16 [2, 2048, 8192], P(None, None, 'mp'), may hold values from -0.125 to 0.125
- bias: float32 [2, 8192], P(None, 'mp'), may hold values from -3 to 3
- w_dec: bfloat16 [2, 2048, 275], P(None, 'mp'), may hold values from -0.75 to 0.75
- b_dec: float32 [2, 275], replicated, may hold values from -3 to 3
Outputs:
- loss: float32 [], replicated
- h_init_grad: float32 [2, 1024, 2048], P(None, 'seq', 'mp')
- c_init_grad: float32 [2, 1024, 2048], P(None, 'seq', 'mp')
- embed_grad: float32 [2, 275, 100], replicated
- w_in_grad: float32 [2, 100, 8192], P(None, None, ('mp', 'seq'))
- w_rec_grad: float32 [2, 2048, 8192], P(None, 'seq', 'mp')
- bias_grad: float32 [2, 8192], P(None, ('mp', 'seq'))
- w_dec_grad: float32 [2, 2048, 275], P(None, ('mp', 'seq'))
- b_dec_grad: float32 [2, 275], replicated
- rms_embed: float32 [2], replicated
- rms_hidden: float32 [2], replicated
- rms_logits: float32 [2], replicated
Inputs may be any that keep to these rules, and one draw needn't show every extreme that they name: `lengths`: they add up to 12288, and the longest stream is valid over all 16 positions. `order`: every stream stands in exactly one slot.
All inputs are finite; a program needn't handle non-finite values.
Results may differ from a plain program's by a relative error of at most 0.018.
Values may be sent and summed in bfloat16 or wider, within the bound.
A program may use at most 256 MiB of HBM per device.

v0:
```python
import jax
import jax.numpy as jnp
from jax import lax
from jax.sharding import PartitionSpec as P


def extended(x, sides, width):
    for axis, dim in sides:
        peers, length = (lax.axis_size(axis), x.shape[dim])
        up = [(i, (i + 1) % peers) for i in range(peers - 1)]
        down = [(j, i) for i, j in up]
        last = lax.slice_in_dim(x, length - width, length, axis=dim)
        leading = lax.slice_in_dim(x, 0, width, axis=dim)
        before = lax.ppermute(last, axis, up)
        after = lax.ppermute(leading, axis, down)
        x = jnp.concatenate([before, x, after], axis=dim)
    return x


def split_gates(pre_gate):
    grouped = pre_gate.reshape(pre_gate.shape[:-1] + (pre_gate.shape[-1] // 4, 4))
    in_gate = jax.nn.sigmoid(grouped[..., 0])
    forget = jax.nn.sigmoid(grouped[..., 1])
    cell_gate = jnp.tanh(grouped[..., 2])
    out_gate = jax.nn.sigmoid(grouped[..., 3])
    return (in_gate, forget, cell_gate, out_gate)


def per_device(ids, lengths, order, h_init, c_init, embed, w_in, w_rec, bias, w_dec, b_dec):
    seq_count = lax.axis_size("seq")
    mp_count = lax.axis_size("mp")
    seq_rank = lax.axis_index("seq")
    mp_rank = lax.axis_index("mp")
    local_time, streams = ids.shape
    length = local_time * seq_count
    per_dev = streams // seq_count
    letter_count = embed.shape[1]
    own_units = w_rec.shape[2] // 4
    all_units = w_rec.shape[1]
    padded = extended(ids, (("seq", 0),), 1)
    slot_pad = jnp.take(padded, order, axis=1)
    slot_ids = slot_pad[1:-1]
    slot_len = jnp.take(lengths, order)
    count = 2.0 * jnp.sum(slot_len - 1).astype(jnp.float32)
    live_total = jnp.sum(slot_len).astype(jnp.float32)
    letters = jnp.arange(letter_count, dtype=jnp.int32)
    onehot = (slot_ids[:, :, None] == letters).astype(jnp.bfloat16)
    letter_rows = jnp.einsum(
        "tbv,dve->tbde", onehot, embed, preferred_element_type=jnp.float32
    ).astype(jnp.bfloat16)
    gates_in = jnp.einsum(
        "tbde,dec->tbdc", letter_rows, w_in, preferred_element_type=jnp.float32
    ).astype(jnp.bfloat16)
    gates_seq = lax.all_to_all(gates_in, "seq", split_axis=1, concat_axis=0, tiled=True)
    own_len = lax.dynamic_slice_in_dim(slot_len, seq_rank * per_dev, per_dev)
    steps = jnp.arange(length, dtype=jnp.int32)

    def step_live(step):
        return jnp.stack([step < own_len, length - 1 - step < own_len])[:, :, None]

    def step_inputs(table, step):
        fore = lax.dynamic_index_in_dim(table, step, 0, keepdims=False)[:, 0]
        back = lax.dynamic_index_in_dim(table, length - 1 - step, 0, keepdims=False)[:, 1]
        return jnp.stack([fore, back])

    def forward_step(carry, step):
        hidden, cell = carry
        whole = lax.all_gather(hidden, "mp", axis=2, tiled=True)
        recurrent = jnp.einsum("dbh,dhc->dbc", whole, w_rec, preferred_element_type=jnp.float32)
        pre_gate = step_inputs(gates_seq, step).astype(jnp.float32) + recurrent + bias[:, None]
        in_gate, forget, cell_gate, out_gate = split_gates(pre_gate)
        new_cell = forget * cell + in_gate * cell_gate
        live = step_live(step)
        cell_next = jnp.where(live, new_cell, cell)
        hidden_next = jnp.where(
            live, out_gate * jnp.tanh(new_cell), hidden.astype(jnp.float32)
        ).astype(jnp.bfloat16)
        return ((hidden_next, cell_next), (hidden, cell, pre_gate, hidden_next))

    final_state, (kept_states, cells, pre_gates, outputs) = lax.scan(
        forward_step, (h_init, c_init), steps
    )
    fore_mask = steps[:, None] < own_len[None, :]
    back_mask = (length - 1 - steps)[:, None] < own_len[None, :]
    live_masks = jnp.stack([fore_mask, back_mask], axis=1).astype(jnp.float32)
    outputs_wide = outputs.astype(jnp.float32)
    hidden_sq_part = jnp.sum(live_masks[..., None] * outputs_wide * outputs_wide, axis=(0, 2, 3))
    time_hidden = jnp.stack([outputs[:, 0], jnp.flip(outputs[:, 1], 0)], axis=2)
    time_major = lax.all_to_all(time_hidden, "seq", split_axis=0, concat_axis=1, tiled=True)
    rows = local_time * streams
    token_hidden = time_major.reshape(rows, 2, own_units)
    tok_dev = rows // mp_count
    piece = token_hidden
    logits = (
        lax.psum_scatter(
            jnp.einsum("rdh,dhv->rdv", piece, w_dec, preferred_element_type=jnp.float32).astype(
                jnp.bfloat16
            ),
            "mp",
            scatter_dimension=0,
            tiled=True,
        ).astype(jnp.float32)
        + b_dec[None]
    )
    first = mp_rank * tok_dev
    ahead = lax.dynamic_slice_in_dim(slot_pad[2:].reshape(rows), first, tok_dev)
    behind = lax.dynamic_slice_in_dim(slot_pad[:-2].reshape(rows), first, tok_dev)
    time_grid = seq_rank * local_time + jnp.arange(local_time, dtype=jnp.int32)[:, None]
    time_rows = lax.dynamic_slice_in_dim(
        jnp.broadcast_to(time_grid, (local_time, streams)).reshape(rows), first, tok_dev
    )
    len_rows = lax.dynamic_slice_in_dim(
        jnp.broadcast_to(slot_len[None, :], (local_time, streams)).reshape(rows), first, tok_dev
    )
    fore_valid = time_rows + 1 < len_rows
    back_valid = (time_rows >= 1) & (time_rows < len_rows)
    valid = jnp.stack([fore_valid, back_valid], axis=1).astype(jnp.float32)
    targets = jnp.stack([ahead, behind], axis=1)
    logit_sq_part = jnp.sum(valid[:, :, None] * logits * logits, axis=(0, 2))
    top = jnp.max(logits, axis=-1, keepdims=True)
    total = jnp.sum(jnp.exp(logits - top), axis=-1, keepdims=True)
    log_total = top + jnp.log(total)
    softmax_out = jnp.exp(logits - log_total)
    target_hot = targets[:, :, None] == letters
    picked = jnp.sum(jnp.where(target_hot, logits, 0.0), axis=-1)
    loss_part = jnp.sum(valid * (log_total[:, :, 0] - picked))
    grad_logits = (
        valid[:, :, None] * (softmax_out - target_hot.astype(jnp.float32)) / count
    ).astype(jnp.bfloat16)
    dec_bias_part = jnp.sum(grad_logits.astype(jnp.float32), axis=0)
    piece = lax.all_gather(grad_logits, "mp", axis=0, tiled=True)
    grad_piece = jnp.einsum("rdv,dhv->rdh", piece, w_dec, preferred_element_type=jnp.float32)
    grad_dec = jnp.einsum("rdh,rdv->dhv", token_hidden, piece, preferred_element_type=jnp.float32)
    grad_from_dec = lax.all_to_all(
        grad_piece.reshape(local_time, streams, 2, own_units).astype(jnp.bfloat16),
        "seq",
        split_axis=1,
        concat_axis=0,
        tiled=True,
    ).astype(jnp.float32)

    def backward_step(carry, inputs):
        grad_hidden, grad_cell = carry
        step, cell, pre_gate = inputs
        grad_hidden = grad_hidden + step_inputs(grad_from_dec, step)
        in_gate, forget, cell_gate, out_gate = split_gates(pre_gate)
        new_cell = forget * cell + in_gate * cell_gate
        squash = jnp.tanh(new_cell)
        live = step_live(step)
        grad_new = jnp.where(
            live, grad_cell + grad_hidden * out_gate * (1.0 - squash * squash), 0.0
        )
        grad_out = jnp.where(live, grad_hidden * squash, 0.0)
        grad_stack = jnp.stack(
            [
                grad_new * cell_gate * in_gate * (1.0 - in_gate),
                grad_new * cell * forget * (1.0 - forget),
                grad_new * in_gate * (1.0 - cell_gate * cell_gate),
                grad_out * out_gate * (1.0 - out_gate),
            ],
            axis=-1,
        )
        grad_pre = grad_stack.reshape(pre_gate.shape).astype(jnp.bfloat16)
        grad_cell_prev = grad_new * forget + jnp.where(live, 0.0, grad_cell)
        held = jnp.where(live, 0.0, grad_hidden)
        terms = jnp.einsum("dbc,dhc->dbh", grad_pre, w_rec, preferred_element_type=jnp.float32)
        through = lax.psum_scatter(
            terms.astype(jnp.bfloat16), "mp", scatter_dimension=2, tiled=True
        ).astype(jnp.float32)
        return ((held + through, grad_cell_prev), grad_pre)

    start_state = jnp.zeros(c_init.shape, jnp.float32)
    (hidden_grad, cell_grad), grad_pres = lax.scan(
        backward_step, (start_state, start_state), (steps, cells, pre_gates), reverse=True
    )
    rec_grad = jnp.einsum(
        "sdbh,sdbc->dhc",
        lax.all_gather(kept_states, "mp", axis=3, tiled=True),
        grad_pres,
        preferred_element_type=jnp.float32,
    )
    gate_bias_grad = jnp.sum(grad_pres.astype(jnp.float32), axis=(0, 2))
    grad_time = jnp.stack([grad_pres[:, 0], jnp.flip(grad_pres[:, 1], 0)], axis=2)
    grad_major = lax.all_to_all(grad_time, "seq", split_axis=0, concat_axis=1, tiled=True)
    in_grad = jnp.einsum(
        "tbde,tbdc->dec", letter_rows, grad_major, preferred_element_type=jnp.float32
    )
    letter_grad = jnp.einsum(
        "tbv,tbdc->dvc", onehot, grad_major, preferred_element_type=jnp.float32
    )
    embed_part = jnp.einsum(
        "dvc,dec->dve", letter_grad, w_in.astype(jnp.float32), precision=lax.Precision.HIGHEST
    )
    rec_part, bias_part, in_part, dec_part = (
        lax.psum_scatter(
            rec_grad.astype(jnp.bfloat16), "seq", scatter_dimension=1, tiled=True
        ).astype(jnp.float32),
        lax.psum_scatter(
            gate_bias_grad.astype(jnp.bfloat16), "seq", scatter_dimension=1, tiled=True
        ).astype(jnp.float32),
        lax.psum_scatter(
            in_grad.astype(jnp.bfloat16), "seq", scatter_dimension=2, tiled=True
        ).astype(jnp.float32),
        lax.psum_scatter(
            grad_dec.astype(jnp.bfloat16), "seq", scatter_dimension=1, tiled=True
        ).astype(jnp.float32),
    )
    loss_sum, hidden_sq, logit_sq, dec_bias_grad, embed_grad = lax.psum(
        (loss_part, hidden_sq_part, logit_sq_part, dec_bias_part, embed_part), ("seq", "mp")
    )
    embed_wide = embed.astype(jnp.float32)
    rms_embed = jnp.sqrt(jnp.mean(embed_wide * embed_wide, axis=(1, 2)))
    rms_hidden = jnp.sqrt(hidden_sq / (all_units * live_total))
    rms_logits = jnp.sqrt(logit_sq / (letter_count * count / 2.0))
    return (
        loss_sum / count,
        hidden_grad,
        cell_grad,
        embed_grad,
        in_part,
        rec_part,
        bias_part,
        dec_part,
        dec_bias_grad,
        rms_embed,
        rms_hidden,
        rms_logits,
    )


def solution(mesh):
    in_specs = (
        P("seq", None),
        P(),
        P(),
        P(None, "seq", "mp"),
        P(None, "seq", "mp"),
        P(),
        P(None, None, "mp"),
        P(None, None, "mp"),
        P(None, "mp"),
        P(None, "mp", None),
        P(),
    )
    out_specs = (
        P(),
        P(None, "seq", "mp"),
        P(None, "seq", "mp"),
        P(),
        P(None, None, ("mp", "seq")),
        P(None, "seq", "mp"),
        P(None, ("mp", "seq")),
        P(None, ("mp", "seq"), None),
        P(),
        P(),
        P(),
        P(),
    )
    return jax.shard_map(
        per_device, mesh=mesh, in_specs=in_specs, out_specs=out_specs, check_vma=False
    )
```

profile of v0, /device:TPU:0, one launch (start us, length us, event | category | flops | bytes accessed | tf_op | source)
XLA Modules:
  0.0 3546.5 jit_solution(18025429574799147192)
XLA Ops:
  65.6 362.8 %all-to-all-done = bf16[4,1024,2,1024]{3,0,2,1:T(4,128)(2,1)} async-done(((bf16[4,1024,2,1024]{3,0,2,1:T(4,128)(2,1)}), bf16[4,1024,2,1024]{3,0,2,1:T(4,128)(2,1)}, u32[]{:S(2)}, u32[]{:S(2)}) %all-to-all-start) | async-done | bytes 16777248 | tf_op jit(solution)/shard_map/all_to_all | solution.py:54
  446.1 767.4 %while.41 = (s32[]{:T(128)}, bf16[2,256,256]{2,1,0:T(8,128)(2,1)S(1)}, f32[2,256,256]{2,1,0:T(8,128)S(1)}, bf16[16,2,256,256]{2,3,0,1:T(8,128)(2,1)}, f32[16,2,2...) while((s32[]{:T(128)}, ...), condition=%wide.region_1.2_spmd, body=%wide.region_0.1_spmd.sunk | while | flops 2152858624 | bytes 51395484 | solution.py:80
  1216.6 98.0 %all_to_all.60 = bf16[16,256,2,256]{3,1,2,0:T(8,128)(2,1)S(1)} all-to-all(bf16[16,256,2,256]{3,1,2,0:T(8,128)(2,1)S(1)} %pad_maximum_fusion.1), channel_id=1, replica_groups=mesh['seq'=4,'mp'=8] {'seq'}, dimensions={0} | all-to-all | bytes 8388608 | tf_op jit(solution)/shard_map/all_to_all | solution.py:89
  1322.7 49.4 %reduce-scatter.9.cloned.1.call-done = bf16[512,2,275]{0,2,1:T(8,128)(2,1)} async-done(((bf16[4096,2,275]{0,2,1:T(8,128)(2,1)}), bf16[512,2,275]{0,2,1:T(8,128)(2,1)}) %reduce-scatter.9.cloned.1.call-update) | async-done | bytes 563216 | tf_op jit(solution)/shard_map/reduce_scatter | solution.py:95
  1433.9 93.9 %all-to-all-done.2 = bf16[4,1024,2,256]{3,0,2,1:T(4,128)(2,1)} async-done(((bf16[4,1024,2,256]{3,0,2,1:T(4,128)(2,1)}), bf16[4,1024,2,256]{3,0,2,1:T(4,128)(2,1)}, u32[]{:S(2)}, u32[]{:S(2)}) %all-to-all-start.2) | async-done | bytes 4194336 | tf_op jit(solution)/shard_map/all_to_all | solution.py:134
  1547.6 1216.8 %while.42 = (s32[]{:T(128)}, f32[2,256,256]{2,1,0:T(8,128)}, f32[2,256,256]{2,1,0:T(8,128)}, bf16[16,2,256,1024]{2,1,3,0:T(2,128)(2,1)}, s32[16]{0:T(128)}, /*in...) while((s32[]{:T(128)}, f32[2,256,256]{2,1,0:T(8,128)}, ...), condition=%wide.region_11.12_spmd.clone, body=%wide.region_9.11_spmd.clone.sunk | while | flops 2157708288 | bytes 57681272 | solution.py:173
  1656.2 39.7 %reduce-scatter.19.cloned.1.call-done = bf16[2,256,256]{2,1,0:T(8,128)(2,1)} async-done(((bf16[2,256,2048]{2,1,0:T(8,128)(2,1)}), bf16[2,256,256]{2,1,0:T(8,128)(2,1)}) %reduce-scatter.19.cloned.1.call-update) | async-done | bytes 262160 | tf_op jit(solution)/shard_map/while/body/eval_jaxpr/reduce_scatter | solution.py:167
  1732.4 39.6 %reduce-scatter.19.cloned.1.call-done = bf16[2,256,256]{2,1,0:T(8,128)(2,1)} async-done(((bf16[2,256,2048]{2,1,0:T(8,128)(2,1)}), bf16[2,256,256]{2,1,0:T(8,128)(2,1)}) %reduce-scatter.19.cloned.1.call-update) | async-done | bytes 262160 | tf_op jit(solution)/shard_map/while/body/eval_jaxpr/reduce_scatter | solution.py:167
  1808.6 39.6 %reduce-scatter.19.cloned.1.call-done = bf16[2,256,256]{2,1,0:T(8,128)(2,1)} async-done(((bf16[2,256,2048]{2,1,0:T(8,128)(2,1)}), bf16[2,256,256]{2,1,0:T(8,128)(2,1)}) %reduce-scatter.19.cloned.1.call-update) | async-done | bytes 262160 | tf_op jit(solution)/shard_map/while/body/eval_jaxpr/reduce_scatter | solution.py:167
  1884.8 39.6 %reduce-scatter.19.cloned.1.call-done = bf16[2,256,256]{2,1,0:T(8,128)(2,1)} async-done(((bf16[2,256,2048]{2,1,0:T(8,128)(2,1)}), bf16[2,256,256]{2,1,0:T(8,128)(2,1)}) %reduce-scatter.19.cloned.1.call-update) | async-done | bytes 262160 | tf_op jit(solution)/shard_map/while/body/eval_jaxpr/reduce_scatter | solution.py:167
  1961.0 39.7 %reduce-scatter.19.cloned.1.call-done = bf16[2,256,256]{2,1,0:T(8,128)(2,1)} async-done(((bf16[2,256,2048]{2,1,0:T(8,128)(2,1)}), bf16[2,256,256]{2,1,0:T(8,128)(2,1)}) %reduce-scatter.19.cloned.1.call-update) | async-done | bytes 262160 | tf_op jit(solution)/shard_map/while/body/eval_jaxpr/reduce_scatter | solution.py:167
  2037.2 39.7 %reduce-scatter.19.cloned.1.call-done = bf16[2,256,256]{2,1,0:T(8,128)(2,1)} async-done(((bf16[2,256,2048]{2,1,0:T(8,128)(2,1)}), bf16[2,256,256]{2,1,0:T(8,128)(2,1)}) %reduce-scatter.19.cloned.1.call-update) | async-done | bytes 262160 | tf_op jit(solution)/shard_map/while/body/eval_jaxpr/reduce_scatter | solution.py:167
  2113.4 39.6 %reduce-scatter.19.cloned.1.call-done = bf16[2,256,256]{2,1,0:T(8,128)(2,1)} async-done(((bf16[2,256,2048]{2,1,0:T(8,128)(2,1)}), bf16[2,256,256]{2,1,0:T(8,128)(2,1)}) %reduce-scatter.19.cloned.1.call-update) | async-done | bytes 262160 | tf_op jit(solution)/shard_map/while/body/eval_jaxpr/reduce_scatter | solution.py:167
  2189.6 39.6 %reduce-scatter.19.cloned.1.call-done = bf16[2,256,256]{2,1,0:T(8,128)(2,1)} async-done(((bf16[2,256,2048]{2,1,0:T(8,128)(2,1)}), bf16[2,256,256]{2,1,0:T(8,128)(2,1)}) %reduce-scatter.19.cloned.1.call-update) | async-done | bytes 262160 | tf_op jit(solution)/shard_map/while/body/eval_jaxpr/reduce_scatter | solution.py:167
  2265.8 39.6 %reduce-scatter.19.cloned.1.call-done = bf16[2,256,256]{2,1,0:T(8,128)(2,1)} async-done(((bf16[2,256,2048]{2,1,0:T(8,128)(2,1)}), bf16[2,256,256]{2,1,0:T(8,128)(2,1)}) %reduce-scatter.19.cloned.1.call-update) | async-done | bytes 262160 | tf_op jit(solution)/shard_map/while/body/eval_jaxpr/reduce_scatter | solution.py:167
  2341.9 39.7 %reduce-scatter.19.cloned.1.call-done = bf16[2,256,256]{2,1,0:T(8,128)(2,1)} async-done(((bf16[2,256,2048]{2,1,0:T(8,128)(2,1)}), bf16[2,256,256]{2,1,0:T(8,128)(2,1)}) %reduce-scatter.19.cloned.1.call-update) | async-done | bytes 262160 | tf_op jit(solution)/shard_map/while/body/eval_jaxpr/reduce_scatter | solution.py:167
  2418.1 39.7 %reduce-scatter.19.cloned.1.call-done = bf16[2,256,256]{2,1,0:T(8,128)(2,1)} async-done(((bf16[2,256,2048]{2,1,0:T(8,128)(2,1)}), bf16[2,256,256]{2,1,0:T(8,128)(2,1)}) %reduce-scatter.19.cloned.1.call-update) | async-done | bytes 262160 | tf_op jit(solution)/shard_map/while/body/eval_jaxpr/reduce_scatter | solution.py:167
  2494.3 39.6 %reduce-scatter.19.cloned.1.call-done = bf16[2,256,256]{2,1,0:T(8,128)(2,1)} async-done(((bf16[2,256,2048]{2,1,0:T(8,128)(2,1)}), bf16[2,256,256]{2,1,0:T(8,128)(2,1)}) %reduce-scatter.19.cloned.1.call-update) | async-done | bytes 262160 | tf_op jit(solution)/shard_map/while/body/eval_jaxpr/reduce_scatter | solution.py:167
  2570.5 39.7 %reduce-scatter.19.cloned.1.call-done = bf16[2,256,256]{2,1,0:T(8,128)(2,1)} async-done(((bf16[2,256,2048]{2,1,0:T(8,128)(2,1)}), bf16[2,256,256]{2,1,0:T(8,128)(2,1)}) %reduce-scatter.19.cloned.1.call-update) | async-done | bytes 262160 | tf_op jit(solution)/shard_map/while/body/eval_jaxpr/reduce_scatter | solution.py:167
  2646.7 39.6 %reduce-scatter.19.cloned.1.call-done = bf16[2,256,256]{2,1,0:T(8,128)(2,1)} async-done(((bf16[2,256,2048]{2,1,0:T(8,128)(2,1)}), bf16[2,256,256]{2,1,0:T(8,128)(2,1)}) %reduce-scatter.19.cloned.1.call-update) | async-done | bytes 262160 | tf_op jit(solution)/shard_map/while/body/eval_jaxpr/reduce_scatter | solution.py:167
  2765.0 41.4 %copy.217 = bf16[16,2,256,1024]{3,2,0,1:T(8,128)(2,1)} copy(bf16[16,2,256,1024]{2,1,3,0:T(2,128)(2,1)} %get-tuple-element.370) | data formatting | bytes 33554432 | tf_op jit(solution)/shard_map/while | solution.py:173
  2877.5 347.3 %all-to-all-done.3 = bf16[16,256,2,1024]{3,1,2,0:T(8,128)(2,1)} async-done(((bf16[16,256,2,1024]{3,1,2,0:T(8,128)(2,1)}), bf16[16,256,2,1024]{3,1,2,0:T(8,128)(2,1)}, u32[]{:S(2)}, u32[]{:S(2)}) %all-to-all-start.3) | async-done | bytes 16777248 | tf_op jit(solution)/shard_map/all_to_all | solution.py:184
  3250.6 42.5 %bitcast_convert_fusion = bf16[2,2048,1024]{2,1,0:T(8,128)(2,1)} fusion(bf16[16,2,256,2048]{2,3,0,1:T(8,128)(2,1)} %all-gather.6.cloned.1.call-done, bf16[16,2,256,1024]{3,2,0,1:T(8,128)(2,1)} %copy.217), kind=kOutput, calls=%fused_computation.73 | convolution fusion | flops 34363932672 | bytes 58720256 | tf_op jit(solution)/shard_map/sdbh,sdbc->dhc/dot_general | solution.py:176
  3390.6 143.3 %reduce-scatter.13.cloned.1.call-done = bf16[2,512,1024]{2,1,0:T(8,128)(2,1)} async-done(((bf16[2,2048,1024]{2,1,0:T(8,128)(2,1)}), bf16[2,512,1024]{2,1,0:T(8,128)(2,1)}) %reduce-scatter.13.cloned.1.call-update) | async-done | bytes 2097168 | tf_op jit(solution)/shard_map/reduce_scatter | solution.py:195
  (1048 shorter events, 1683.0 us)
Async XLA Ops:
  57.6 370.8 %all-to-all-start = ((bf16[4,1024,2,1024]{3,0,2,1:T(4,128)(2,1)}), bf16[4,1024,2,1024]{3,0,2,1:T(4,128)(2,1)}, u32[]{:S(2)}, u32[]{:S(2)}) async-start(bf16[4,1024,2,1024]{3,0,2,1:T(4,128)(2,1)} %copy.205), calls=%async_computation.1 | async-start | bytes 33554432 | tf_op jit(solution)/shard_map/all_to_all | solution.py:54
  1213.5 158.6 %reduce-scatter.9.cloned.1.call-start = ((), (), s32[]{:S(2)}) async-start(), calls=%async_computation.10 | async-start | bytes 5160960 | tf_op jit(solution)/shard_map/reduce_scatter | solution.py:95
  1320.7 97.7 %all-gather.4.cloned.1.call-start = ((), (), s32[]{:S(2)}) async-start(), calls=%async_computation.11 | async-start | bytes 5160960 | tf_op jit(solution)/shard_map/all_gather | solution.py:131
  1428.7 99.0 %all-to-all-start.2 = ((bf16[4,1024,2,256]{3,0,2,1:T(4,128)(2,1)}), bf16[4,1024,2,256]{3,0,2,1:T(4,128)(2,1)}, u32[]{:S(2)}, u32[]{:S(2)}) async-start(bf16[4,1024,2,256]{3,0,2,1:T(4,128)(2,1)} %copy.214), calls=%async_computation.4 | async-start | bytes 8388608 | tf_op jit(solution)/shard_map/all_to_all | solution.py:134
  1621.6 74.3 %reduce-scatter.19.cloned.1.call-start = ((), (), s32[]{:S(2)}) async-start(), calls=%async_computation.19 | async-start | bytes 2359296 | tf_op jit(solution)/shard_map/while/body/eval_jaxpr/reduce_scatter | solution.py:167
  1697.8 74.3 %reduce-scatter.19.cloned.1.call-start = ((), (), s32[]{:S(2)}) async-start(), calls=%async_computation.19 | async-start | bytes 2359296 | tf_op jit(solution)/shard_map/while/body/eval_jaxpr/reduce_scatter | solution.py:167
  1773.9 74.3 %reduce-scatter.19.cloned.1.call-start = ((), (), s32[]{:S(2)}) async-start(), calls=%async_computation.19 | async-start | bytes 2359296 | tf_op jit(solution)/shard_map/while/body/eval_jaxpr/reduce_scatter | solution.py:167
  1850.1 74.3 %reduce-scatter.19.cloned.1.call-start = ((), (), s32[]{:S(2)}) async-start(), calls=%async_computation.19 | async-start | bytes 2359296 | tf_op jit(solution)/shard_map/while/body/eval_jaxpr/reduce_scatter | solution.py:167
  1926.3 74.3 %reduce-scatter.19.cloned.1.call-start = ((), (), s32[]{:S(2)}) async-start(), calls=%async_computation.19 | async-start | bytes 2359296 | tf_op jit(solution)/shard_map/while/body/eval_jaxpr/reduce_scatter | solution.py:167
  2002.5 74.3 %reduce-scatter.19.cloned.1.call-start = ((), (), s32[]{:S(2)}) async-start(), calls=%async_computation.19 | async-start | bytes 2359296 | tf_op jit(solution)/shard_map/while/body/eval_jaxpr/reduce_scatter | solution.py:167
  2078.7 74.3 %reduce-scatter.19.cloned.1.call-start = ((), (), s32[]{:S(2)}) async-start(), calls=%async_computation.19 | async-start | bytes 2359296 | tf_op jit(solution)/shard_map/while/body/eval_jaxpr/reduce_scatter | solution.py:167
  2231.1 74.3 %reduce-scatter.19.cloned.1.call-start = ((), (), s32[]{:S(2)}) async-start(), calls=%async_computation.19 | async-start | bytes 2359296 | tf_op jit(solution)/shard_map/while/body/eval_jaxpr/reduce_scatter | solution.py:167
  2307.3 74.3 %reduce-scatter.19.cloned.1.call-start = ((), (), s32[]{:S(2)}) async-start(), calls=%async_computation.19 | async-start | bytes 2359296 | tf_op jit(solution)/shard_map/while/body/eval_jaxpr/reduce_scatter | solution.py:167
  2383.5 74.3 %reduce-scatter.19.cloned.1.call-start = ((), (), s32[]{:S(2)}) async-start(), calls=%async_computation.19 | async-start | bytes 2359296 | tf_op jit(solution)/shard_map/while/body/eval_jaxpr/reduce_scatter | solution.py:167
  2459.6 74.3 %reduce-scatter.19.cloned.1.call-start = ((), (), s32[]{:S(2)}) async-start(), calls=%async_computation.19 | async-start | bytes 2359296 | tf_op jit(solution)/shard_map/while/body/eval_jaxpr/reduce_scatter | solution.py:167
  2535.8 74.3 %reduce-scatter.19.cloned.1.call-start = ((), (), s32[]{:S(2)}) async-start(), calls=%async_computation.19 | async-start | bytes 2359296 | tf_op jit(solution)/shard_map/while/body/eval_jaxpr/reduce_scatter | solution.py:167
  2688.2 74.3 %reduce-scatter.19.cloned.1.call-start = ((), (), s32[]{:S(2)}) async-start(), calls=%async_computation.19 | async-start | bytes 2359296 | tf_op jit(solution)/shard_map/while/body/eval_jaxpr/reduce_scatter | solution.py:167
  2764.4 486.2 %all-gather.6.cloned.1.call-start = ((), (), s32[]{:S(2)}) async-start(), calls=%async_computation.14 | async-start | bytes 37748736 | tf_op jit(solution)/shard_map/all_gather | solution.py:178
  2843.8 381.0 %all-to-all-start.3 = ((bf16[16,256,2,1024]{3,1,2,0:T(8,128)(2,1)}), bf16[16,256,2,1024]{3,1,2,0:T(8,128)(2,1)}, u32[]{:S(2)}, u32[]{:S(2)}) async-start(bf16[16,256,2,1024]{3,1,2,0:T(8,128)(2,1)} %copy.219), calls=%async_computation.5 | async-start | bytes 33554432 | tf_op jit(solution)/shard_map/all_to_all | solution.py:184
  2851.0 487.5 %reduce-scatter.15.cloned.1.call-start = ((), (), s32[]{:S(2)}) async-start(), calls=%async_computation.16 | async-start | bytes 491520 | tf_op jit(solution)/shard_map/reduce_scatter | solution.py:204
  2858.3 481.8 %reduce-scatter.17.cloned.1.call-start = ((), (), s32[]{:S(2)}) async-start(), calls=%async_computation.17 | async-start | bytes 327680
  2877.2 487.7 %all-reduce.3.cloned.1.call-start = ((), (), s32[]{:S(2)}) async-start(), calls=%async_computation.12 | async-start | bytes 573440 | tf_op jit(solution)/shard_map/psum | solution.py:208
  3241.1 147.9 %reduce-scatter.11.cloned.1.call-start = ((), (), s32[]{:S(2)}) async-start(), calls=%async_computation.13 | async-start | bytes 532480 | tf_op jit(solution)/shard_map/reduce_scatter | solution.py:201
  3250.3 283.6 %reduce-scatter.13.cloned.1.call-start = ((), (), s32[]{:S(2)}) async-start(), calls=%async_computation.15 | async-start | bytes 10485760 | tf_op jit(solution)/shard_map/reduce_scatter | solution.py:195
  (123 other events, 1897.1 us)
Sparse Core Ops, SparseCore 0:
  496.6 28.1 all-gather.7
  544.7 28.1 all-gather.7
  784.8 28.1 all-gather.7
  832.9 28.1 all-gather.7
  880.7 28.1 all-gather.7
  1072.9 28.1 all-gather.7
  1120.8 28.1 all-gather.7
  1168.6 28.1 all-gather.7
  1580.3 39.3 reduce-scatter.18
  1654.6 41.2 reduce-scatter.18
  1730.8 41.2 reduce-scatter.18
  1807.0 41.2 reduce-scatter.18
  1883.2 41.2 reduce-scatter.18
  1959.4 41.2 reduce-scatter.18
  2035.6 41.2 reduce-scatter.18
  2111.8 41.2 reduce-scatter.18
  2188.0 41.1 reduce-scatter.18
  2264.1 41.1 reduce-scatter.18
  2340.3 41.2 reduce-scatter.18
  2416.5 41.2 reduce-scatter.18
  2492.7 41.2 reduce-scatter.18
  2568.9 41.2 reduce-scatter.18
  2645.1 41.2 reduce-scatter.18
  2721.3 41.2 reduce-scatter.18
  (8 shorter events, 224.1 us)
Sparse Core Ops, SparseCore 1:
  1320.8 51.3 reduce-scatter.8
  1379.4 38.9 all-gather.3
  2767.3 160.6 all-gather.5
  2930.3 28.1 reduce-scatter.14
  2961.4 191.8 reduce-scatter.16
  3241.2 123.7 all-reduce.2
  3367.2 21.7 reduce-scatter.10
  3391.2 142.7 reduce-scatter.12
where the time goes:
time: 3560 us; the launch traced here: 3550 us
  waiting for transfers between devices  2020 us (57%)
  local copies, waits for them, and re-layouts  670 us (19%)
  matrix products  324 us (9%)
  other arithmetic  243 us (7%)
  blocking collectives  136 us (4%)
  loops' own time  111 us (3%)
    reduce_scatter x16, waiting for transfers between devices, backward_step(): lax.psum_scatter(terms.astype(jnp.bfloat16), 'mp', scatter_dimension=2, t...  632 us
    all_to_all x1, waiting for transfers between devices, per_device(): lax.all_to_all(gates_in, 'seq', split_axis=1, concat_axis=0, tiled=True)  363 us
    all_to_all x1, waiting for transfers between devices, per_device(): lax.all_to_all(grad_time, 'seq', split_axis=0, concat_axis=1, tiled=True)  347 us
    all_gather x16, waiting for transfers between devices, forward_step(): whole = lax.all_gather(hidden, 'mp', axis=2, tiled=True)  302 us
    reduce_scatter x1, waiting for transfers between devices, per_device(): lax.psum_scatter(rec_grad.astype(jnp.bfloat16), 'seq', scatter_dimension=...  143 us
    dot_general x16, matrix products, forward_step(): jnp.einsum('dbh,dhc->dbc', whole, w_rec, preferred_element_type=jnp.float32)  124 us
    dot_general x16, matrix products, backward_step(): jnp.einsum('dbc,dhc->dbh', grad_pre, w_rec, preferred_element_type=jnp.fl...  115 us
    all_to_all x1, blocking collectives, per_device(): lax.all_to_all(time_hidden, 'seq', split_axis=0, concat_axis=1, tiled=True)  98 us
  transfers between devices with their start and end apart: 45, of which 40 were waited for; matrix products, arithmetic and copies ran while one was open for 10% of the time, Pallas kernels for 0%

commit v1 on v0

--- a/solution.py
+++ b/solution.py
@@ -131,12 +131,20 @@
     piece = lax.all_gather(grad_logits, "mp", axis=0, tiled=True)
     grad_piece = jnp.einsum("rdv,dhv->rdh", piece, w_dec, preferred_element_type=jnp.float32)
     grad_dec = jnp.einsum("rdh,rdv->dhv", token_hidden, piece, preferred_element_type=jnp.float32)
-    grad_from_dec = lax.all_to_all(
-        grad_piece.reshape(local_time, streams, 2, own_units).astype(jnp.bfloat16),
-        "seq",
-        split_axis=1,
-        concat_axis=0,
-        tiled=True,
+    grad_from_dec = jnp.concatenate(
+        lax.all_to_all(
+            jnp.stack(
+                jnp.split(
+                    grad_piece.reshape(local_time, streams, 2, own_units).astype(jnp.bfloat16),
+                    lax.axis_size("seq"),
+                    axis=1,
+                )
+            ),
+            "seq",
+            0,
+            0,
+        ),
+        axis=0,
     ).astype(jnp.float32)
 
     def backward_step(carry, inputs):

time: 3560 us -> 3550 us (level)
  no operation moved by 1% of the time
where the time goes in v1:
time: 3550 us; the launch traced here: 3530 us
  waiting for transfers between devices  2020 us (57%)
  local copies, waits for them, and re-layouts  666 us (19%)
  matrix products  324 us (9%)
  other arithmetic  241 us (7%)
  blocking collectives  136 us (4%)
  loops' own time  106 us (3%)
    reduce_scatter x16, waiting for transfers between devices, backward_step(): lax.psum_scatter(terms.astype(jnp.bfloat16), 'mp', scatter_dimension=2, t...  633 us
    all_to_all x1, waiting for transfers between devices, per_device(): lax.all_to_all(gates_in, 'seq', split_axis=1, concat_axis=0, tiled=True)  363 us
    all_to_all x1, waiting for transfers between devices, per_device(): lax.all_to_all(grad_time, 'seq', split_axis=0, concat_axis=1, tiled=True)  347 us
    all_gather x16, waiting for transfers between devices, forward_step(): whole = lax.all_gather(hidden, 'mp', axis=2, tiled=True)  302 us
    reduce_scatter x1, waiting for transfers between devices, per_device(): lax.psum_scatter(rec_grad.astype(jnp.bfloat16), 'seq', scatter_dimension=...  143 us
    dot_general x16, matrix products, forward_step(): jnp.einsum('dbh,dhc->dbc', whole, w_rec, preferred_element_type=jnp.float32)  124 us
    dot_general x16, matrix products, backward_step(): jnp.einsum('dbc,dhc->dbh', grad_pre, w_rec, preferred_element_type=jnp.fl...  115 us
    all_to_all x1, blocking collectives, per_device(): lax.all_to_all(time_hidden, 'seq', split_axis=0, concat_axis=1, tiled=True)  98 us
  transfers between devices with their start and end apart: 45, of which 40 were waited for; matrix products, arithmetic and copies ran while one was open for 10% of the time, Pallas kernels for 0%

profile of v1, /device:TPU:0, one launch (start us, length us, event | category | flops | bytes accessed | tf_op | source)
XLA Modules:
  0.0 3534.5 jit_solution(1994453435625389907)
XLA Ops:
  65.6 362.8 %all-to-all-done = bf16[4,1024,2,1024]{3,0,2,1:T(4,128)(2,1)} async-done(((bf16[4,1024,2,1024]{3,0,2,1:T(4,128)(2,1)}), bf16[4,1024,2,1024]{3,0,2,1:T(4,128)(2,1)}, u32[]{:S(2)}, u32[]{:S(2)}) %all-to-all-start) | async-done | bytes 16777248 | tf_op jit(solution)/shard_map/all_to_all | solution.py:54
  446.0 767.3 %while.41 = (s32[]{:T(128)}, bf16[2,256,256]{2,1,0:T(8,128)(2,1)S(1)}, f32[2,256,256]{2,1,0:T(8,128)S(1)}, bf16[16,2,256,256]{2,3,0,1:T(8,128)(2,1)}, f32[16,2,2...) while((s32[]{:T(128)}, ...), condition=%wide.region_1.2_spmd, body=%wide.region_0.1_spmd.sunk | while | flops 2152858624 | bytes 51395484 | solution.py:80
  1216.5 98.0 %all_to_all.56 = bf16[16,256,2,256]{3,1,2,0:T(8,128)(2,1)S(1)} all-to-all(bf16[16,256,2,256]{3,1,2,0:T(8,128)(2,1)S(1)} %pad_maximum_fusion.1), channel_id=1, replica_groups=mesh['seq'=4,'mp'=8] {'seq'}, dimensions={0} | all-to-all | bytes 8388608 | tf_op jit(solution)/shard_map/all_to_all | solution.py:89
  1322.6 49.4 %reduce-scatter.9.cloned.1.call-done = bf16[512,2,275]{0,2,1:T(8,128)(2,1)} async-done(((bf16[4096,2,275]{0,2,1:T(8,128)(2,1)}), bf16[512,2,275]{0,2,1:T(8,128)(2,1)}) %reduce-scatter.9.cloned.1.call-update) | async-done | bytes 563216 | tf_op jit(solution)/shard_map/reduce_scatter | solution.py:95
  1430.8 93.9 %all-to-all-done.2 = bf16[4,4,256,2,256]{4,2,1,3,0:T(8,128)(2,1)} async-done(((bf16[4,4,256,2,256]{4,2,1,3,0:T(8,128)(2,1)}), bf16[4,4,256,2,256]{4,2,1,3,0:T(8,128)(2,1)}, u32[]{:S(2)}, u32[]{:S(2)}) %all-to-all-start.2) | async-done | bytes 4194336 | tf_op jit(solution)/shard_map/all_to_all | solution.py:135
  1541.9 1210.5 %while.42 = (s32[]{:T(128)}, f32[2,256,256]{2,1,0:T(8,128)}, f32[2,256,256]{2,1,0:T(8,128)}, bf16[16,2,256,1024]{2,1,3,0:T(2,128)(2,1)}, s32[16]{0:T(128)}, /*in...) while((s32[]{:T(128)}, f32[2,256,256]{2,1,0:T(8,128)}, ...), condition=%wide.region_11.12_spmd.clone, body=%wide.region_9.11_spmd.clone.sunk | while | flops 2157708288 | bytes 57681272 | solution.py:181
  1649.7 39.7 %reduce-scatter.19.cloned.1.call-done = bf16[2,256,256]{2,1,0:T(8,128)(2,1)} async-done(((bf16[2,256,2048]{2,1,0:T(8,128)(2,1)}), bf16[2,256,256]{2,1,0:T(8,128)(2,1)}) %reduce-scatter.19.cloned.1.call-update) | async-done | bytes 262160 | tf_op jit(solution)/shard_map/while/body/eval_jaxpr/reduce_scatter | solution.py:175
  1725.6 39.6 %reduce-scatter.19.cloned.1.call-done = bf16[2,256,256]{2,1,0:T(8,128)(2,1)} async-done(((bf16[2,256,2048]{2,1,0:T(8,128)(2,1)}), bf16[2,256,256]{2,1,0:T(8,128)(2,1)}) %reduce-scatter.19.cloned.1.call-update) | async-done | bytes 262160 | tf_op jit(solution)/shard_map/while/body/eval_jaxpr/reduce_scatter | solution.py:175
  1877.1 39.6 %reduce-scatter.19.cloned.1.call-done = bf16[2,256,256]{2,1,0:T(8,128)(2,1)} async-done(((bf16[2,256,2048]{2,1,0:T(8,128)(2,1)}), bf16[2,256,256]{2,1,0:T(8,128)(2,1)}) %reduce-scatter.19.cloned.1.call-update) | async-done | bytes 262160 | tf_op jit(solution)/shard_map/while/body/eval_jaxpr/reduce_scatter | solution.py:175
  1952.9 39.7 %reduce-scatter.19.cloned.1.call-done = bf16[2,256,256]{2,1,0:T(8,128)(2,1)} async-done(((bf16[2,256,2048]{2,1,0:T(8,128)(2,1)}), bf16[2,256,256]{2,1,0:T(8,128)(2,1)}) %reduce-scatter.19.cloned.1.call-update) | async-done | bytes 262160 | tf_op jit(solution)/shard_map/while/body/eval_jaxpr/reduce_scatter | solution.py:175
  2028.7 39.7 %reduce-scatter.19.cloned.1.call-done = bf16[2,256,256]{2,1,0:T(8,128)(2,1)} async-done(((bf16[2,256,2048]{2,1,0:T(8,128)(2,1)}), bf16[2,256,256]{2,1,0:T(8,128)(2,1)}) %reduce-scatter.19.cloned.1.call-update) | async-done | bytes 262160 | tf_op jit(solution)/shard_map/while/body/eval_jaxpr/reduce_scatter | solution.py:175
  2104.5 39.6 %reduce-scatter.19.cloned.1.call-done = bf16[2,256,256]{2,1,0:T(8,128)(2,1)} async-done(((bf16[2,256,2048]{2,1,0:T(8,128)(2,1)}), bf16[2,256,256]{2,1,0:T(8,128)(2,1)}) %reduce-scatter.19.cloned.1.call-update) | async-done | bytes 262160 | tf_op jit(solution)/shard_map/while/body/eval_jaxpr/reduce_scatter | solution.py:175
  2180.3 39.6 %reduce-scatter.19.cloned.1.call-done = bf16[2,256,256]{2,1,0:T(8,128)(2,1)} async-done(((bf16[2,256,2048]{2,1,0:T(8,128)(2,1)}), bf16[2,256,256]{2,1,0:T(8,128)(2,1)}) %reduce-scatter.19.cloned.1.call-update) | async-done | bytes 262160 | tf_op jit(solution)/shard_map/while/body/eval_jaxpr/reduce_scatter | solution.py:175
  2256.1 39.6 %reduce-scatter.19.cloned.1.call-done = bf16[2,256,256]{2,1,0:T(8,128)(2,1)} async-done(((bf16[2,256,2048]{2,1,0:T(8,128)(2,1)}), bf16[2,256,256]{2,1,0:T(8,128)(2,1)}) %reduce-scatter.19.cloned.1.call-update) | async-done | bytes 262160 | tf_op jit(solution)/shard_map/while/body/eval_jaxpr/reduce_scatter | solution.py:175
  2331.8 39.7 %reduce-scatter.19.cloned.1.call-done = bf16[2,256,256]{2,1,0:T(8,128)(2,1)} async-done(((bf16[2,256,2048]{2,1,0:T(8,128)(2,1)}), bf16[2,256,256]{2,1,0:T(8,128)(2,1)}) %reduce-scatter.19.cloned.1.call-update) | async-done | bytes 262160 | tf_op jit(solution)/shard_map/while/body/eval_jaxpr/reduce_scatter | solution.py:175
  2407.6 39.7 %reduce-scatter.19.cloned.1.call-done = bf16[2,256,256]{2,1,0:T(8,128)(2,1)} async-done(((bf16[2,256,2048]{2,1,0:T(8,128)(2,1)}), bf16[2,256,256]{2,1,0:T(8,128)(2,1)}) %reduce-scatter.19.cloned.1.call-update) | async-done | bytes 262160 | tf_op jit(solution)/shard_map/while/body/eval_jaxpr/reduce_scatter | solution.py:175
  2483.4 39.7 %reduce-scatter.19.cloned.1.call-done = bf16[2,256,256]{2,1,0:T(8,128)(2,1)} async-done(((bf16[2,256,2048]{2,1,0:T(8,128)(2,1)}), bf16[2,256,256]{2,1,0:T(8,128)(2,1)}) %reduce-scatter.19.cloned.1.call-update) | async-done | bytes 262160 | tf_op jit(solution)/shard_map/while/body/eval_jaxpr/reduce_scatter | solution.py:175
  2559.2 39.7 %reduce-scatter.19.cloned.1.call-done = bf16[2,256,256]{2,1,0:T(8,128)(2,1)} async-done(((bf16[2,256,2048]{2,1,0:T(8,128)(2,1)}), bf16[2,256,256]{2,1,0:T(8,128)(2,1)}) %reduce-scatter.19.cloned.1.call-update) | async-done | bytes 262160 | tf_op jit(solution)/shard_map/while/body/eval_jaxpr/reduce_scatter | solution.py:175
  2635.0 39.7 %reduce-scatter.19.cloned.1.call-done = bf16[2,256,256]{2,1,0:T(8,128)(2,1)} async-done(((bf16[2,256,2048]{2,1,0:T(8,128)(2,1)}), bf16[2,256,256]{2,1,0:T(8,128)(2,1)}) %reduce-scatter.19.cloned.1.call-update) | async-done | bytes 262160 | tf_op jit(solution)/shard_map/while/body/eval_jaxpr/reduce_scatter | solution.py:175
  2710.9 39.6 %reduce-scatter.19.cloned.1.call-done = bf16[2,256,256]{2,1,0:T(8,128)(2,1)} async-done(((bf16[2,256,2048]{2,1,0:T(8,128)(2,1)}), bf16[2,256,256]{2,1,0:T(8,128)(2,1)}) %reduce-scatter.19.cloned.1.call-update) | async-done | bytes 262160 | tf_op jit(solution)/shard_map/while/body/eval_jaxpr/reduce_scatter | solution.py:175
  2753.0 41.4 %copy.215 = bf16[16,2,256,1024]{3,2,0,1:T(8,128)(2,1)} copy(bf16[16,2,256,1024]{2,1,3,0:T(2,128)(2,1)} %get-tuple-element.370) | data formatting | bytes 33554432 | tf_op jit(solution)/shard_map/while | solution.py:181
  2865.7 347.0 %all-to-all-done.3 = bf16[16,256,2,1024]{3,1,2,0:T(8,128)(2,1)} async-done(((bf16[16,256,2,1024]{3,1,2,0:T(8,128)(2,1)}), bf16[16,256,2,1024]{3,1,2,0:T(8,128)(2,1)}, u32[]{:S(2)}, u32[]{:S(2)}) %all-to-all-start.3) | async-done | bytes 16777248 | tf_op jit(solution)/shard_map/all_to_all | solution.py:192
  3238.5 42.5 %bitcast_convert_fusion = bf16[2,2048,1024]{2,1,0:T(8,128)(2,1)} fusion(bf16[16,2,256,2048]{2,3,0,1:T(8,128)(2,1)} %all-gather.6.cloned.1.call-done, bf16[16,2,256,1024]{3,2,0,1:T(8,128)(2,1)} %copy.215), kind=kOutput, calls=%fused_computation.73 | convolution fusion | flops 34363932672 | bytes 58720256 | tf_op jit(solution)/shard_map/sdbh,sdbc->dhc/dot_general | solution.py:184
  3378.7 143.3 %reduce-scatter.13.cloned.1.call-done = bf16[2,512,1024]{2,1,0:T(8,128)(2,1)} async-done(((bf16[2,2048,1024]{2,1,0:T(8,128)(2,1)}), bf16[2,512,1024]{2,1,0:T(8,128)(2,1)}) %reduce-scatter.13.cloned.1.call-update) | async-done | bytes 2097168 | tf_op jit(solution)/shard_map/reduce_scatter | solution.py:203
  (1048 shorter events, 1676.5 us)
Async XLA Ops:
  57.6 370.8 %all-to-all-start = ((bf16[4,1024,2,1024]{3,0,2,1:T(4,128)(2,1)}), bf16[4,1024,2,1024]{3,0,2,1:T(4,128)(2,1)}, u32[]{:S(2)}, u32[]{:S(2)}) async-start(bf16[4,1024,2,1024]{3,0,2,1:T(4,128)(2,1)} %copy.204), calls=%async_computation.1 | async-start | bytes 33554432 | tf_op jit(solution)/shard_map/all_to_all | solution.py:54
  1213.3 158.6 %reduce-scatter.9.cloned.1.call-start = ((), (), s32[]{:S(2)}) async-start(), calls=%async_computation.10 | async-start | bytes 5160960 | tf_op jit(solution)/shard_map/reduce_scatter | solution.py:95
  1320.6 97.7 %all-gather.4.cloned.1.call-start = ((), (), s32[]{:S(2)}) async-start(), calls=%async_computation.11 | async-start | bytes 5160960 | tf_op jit(solution)/shard_map/all_gather | solution.py:131
  1426.0 98.8 %all-to-all-start.2 = ((bf16[4,4,256,2,256]{4,2,1,3,0:T(8,128)(2,1)}), bf16[4,4,256,2,256]{4,2,1,3,0:T(8,128)(2,1)}, u32[]{:S(2)}, u32[]{:S(2)}) async-start(bf16[4,4,256,2,256]{4,2,1,3,0:T(8,128)(2,1)} %pad_maximum_fusion.2), calls=%async_computation.4 | async-start | bytes 8388608 | tf_op jit(solution)/shard_map/all_to_all | solution.py:135
  1615.5 73.9 %reduce-scatter.19.cloned.1.call-start = ((), (), s32[]{:S(2)}) async-start(), calls=%async_computation.19 | async-start | bytes 2359296 | tf_op jit(solution)/shard_map/while/body/eval_jaxpr/reduce_scatter | solution.py:175
  1691.3 73.9 %reduce-scatter.19.cloned.1.call-start = ((), (), s32[]{:S(2)}) async-start(), calls=%async_computation.19 | async-start | bytes 2359296 | tf_op jit(solution)/shard_map/while/body/eval_jaxpr/reduce_scatter | solution.py:175
  1767.1 73.9 %reduce-scatter.19.cloned.1.call-start = ((), (), s32[]{:S(2)}) async-start(), calls=%async_computation.19 | async-start | bytes 2359296 | tf_op jit(solution)/shard_map/while/body/eval_jaxpr/reduce_scatter | solution.py:175
  1842.9 73.9 %reduce-scatter.19.cloned.1.call-start = ((), (), s32[]{:S(2)}) async-start(), calls=%async_computation.19 | async-start | bytes 2359296 | tf_op jit(solution)/shard_map/while/body/eval_jaxpr/reduce_scatter | solution.py:175
  1918.7 73.9 %reduce-scatter.19.cloned.1.call-start = ((), (), s32[]{:S(2)}) async-start(), calls=%async_computation.19 | async-start | bytes 2359296 | tf_op jit(solution)/shard_map/while/body/eval_jaxpr/reduce_scatter | solution.py:175
  1994.5 73.9 %reduce-scatter.19.cloned.1.call-start = ((), (), s32[]{:S(2)}) async-start(), calls=%async_computation.19 | async-start | bytes 2359296 | tf_op jit(solution)/shard_map/while/body/eval_jaxpr/reduce_scatter | solution.py:175
  2070.2 73.9 %reduce-scatter.19.cloned.1.call-start = ((), (), s32[]{:S(2)}) async-start(), calls=%async_computation.19 | async-start | bytes 2359296 | tf_op jit(solution)/shard_map/while/body/eval_jaxpr/reduce_scatter | solution.py:175
  2146.0 73.9 %reduce-scatter.19.cloned.1.call-start = ((), (), s32[]{:S(2)}) async-start(), calls=%async_computation.19 | async-start | bytes 2359296 | tf_op jit(solution)/shard_map/while/body/eval_jaxpr/reduce_scatter | solution.py:175
  2221.8 73.9 %reduce-scatter.19.cloned.1.call-start = ((), (), s32[]{:S(2)}) async-start(), calls=%async_computation.19 | async-start | bytes 2359296 | tf_op jit(solution)/shard_map/while/body/eval_jaxpr/reduce_scatter | solution.py:175
  2449.2 73.9 %reduce-scatter.19.cloned.1.call-start = ((), (), s32[]{:S(2)}) async-start(), calls=%async_computation.19 | async-start | bytes 2359296 | tf_op jit(solution)/shard_map/while/body/eval_jaxpr/reduce_scatter | solution.py:175
  2525.0 73.9 %reduce-scatter.19.cloned.1.call-start = ((), (), s32[]{:S(2)}) async-start(), calls=%async_computation.19 | async-start | bytes 2359296 | tf_op jit(solution)/shard_map/while/body/eval_jaxpr/reduce_scatter | solution.py:175
  2600.8 73.9 %reduce-scatter.19.cloned.1.call-start = ((), (), s32[]{:S(2)}) async-start(), calls=%async_computation.19 | async-start | bytes 2359296 | tf_op jit(solution)/shard_map/while/body/eval_jaxpr/reduce_scatter | solution.py:175
  2676.6 73.9 %reduce-scatter.19.cloned.1.call-start = ((), (), s32[]{:S(2)}) async-start(), calls=%async_computation.19 | async-start | bytes 2359296 | tf_op jit(solution)/shard_map/while/body/eval_jaxpr/reduce_scatter | solution.py:175
  2752.4 486.1 %all-gather.6.cloned.1.call-start = ((), (), s32[]{:S(2)}) async-start(), calls=%async_computation.14 | async-start | bytes 37748736 | tf_op jit(solution)/shard_map/all_gather | solution.py:186
  2831.7 381.0 %all-to-all-start.3 = ((bf16[16,256,2,1024]{3,1,2,0:T(8,128)(2,1)}), bf16[16,256,2,1024]{3,1,2,0:T(8,128)(2,1)}, u32[]{:S(2)}, u32[]{:S(2)}) async-start(bf16[16,256,2,1024]{3,1,2,0:T(8,128)(2,1)} %copy.217), calls=%async_computation.5 | async-start | bytes 33554432 | tf_op jit(solution)/shard_map/all_to_all | solution.py:192
  2839.0 487.5 %reduce-scatter.15.cloned.1.call-start = ((), (), s32[]{:S(2)}) async-start(), calls=%async_computation.16 | async-start | bytes 491520 | tf_op jit(solution)/shard_map/reduce_scatter | solution.py:212
  2846.8 481.3 %reduce-scatter.17.cloned.1.call-start = ((), (), s32[]{:S(2)}) async-start(), calls=%async_computation.17 | async-start | bytes 327680
  2865.7 487.3 %all-reduce.3.cloned.1.call-start = ((), (), s32[]{:S(2)}) async-start(), calls=%async_computation.12 | async-start | bytes 573440 | tf_op jit(solution)/shard_map/psum | solution.py:216
  3229.0 148.0 %reduce-scatter.11.cloned.1.call-start = ((), (), s32[]{:S(2)}) async-start(), calls=%async_computation.13 | async-start | bytes 532480 | tf_op jit(solution)/shard_map/reduce_scatter | solution.py:209
  3238.5 283.5 %reduce-scatter.13.cloned.1.call-start = ((), (), s32[]{:S(2)}) async-start(), calls=%async_computation.15 | async-start | bytes 10485760 | tf_op jit(solution)/shard_map/reduce_scatter | solution.py:203
  (123 other events, 1896.2 us)
Sparse Core Ops, SparseCore 0:
  496.5 28.1 all-gather.7
  688.3 28.1 all-gather.7
  736.6 28.1 all-gather.7
  784.7 28.1 all-gather.7
  880.7 28.1 all-gather.7
  928.8 28.1 all-gather.7
  1024.9 28.1 all-gather.7
  1120.7 28.1 all-gather.7
  1574.2 39.3 reduce-scatter.18
  1648.2 41.2 reduce-scatter.18
  1724.0 41.2 reduce-scatter.18
  1799.7 41.2 reduce-scatter.18
  1875.5 41.2 reduce-scatter.18
  1951.3 41.2 reduce-scatter.18
  2027.1 41.2 reduce-scatter.18
  2102.9 41.2 reduce-scatter.18
  2178.7 41.2 reduce-scatter.18
  2254.5 41.2 reduce-scatter.18
  2330.3 41.2 reduce-scatter.18
  2406.1 41.2 reduce-scatter.18
  2481.8 41.2 reduce-scatter.18
  2557.6 41.2 reduce-scatter.18
  2633.4 41.2 reduce-scatter.18
  2709.3 41.2 reduce-scatter.18
  (8 shorter events, 224.1 us)
Sparse Core Ops, SparseCore 1:
  1320.7 51.3 reduce-scatter.8
  1379.2 38.9 all-gather.3
  2755.4 160.6 all-gather.5
  2918.3 28.0 reduce-scatter.14
  2949.4 191.9 reduce-scatter.16
  3229.1 123.8 all-reduce.2
  3355.2 21.7 reduce-scatter.10
  3379.2 142.7 reduce-scatter.12
